TPU v7x, 32 devices: a whole 2x2x4 slice. The times are simulated.
32 devices in a mesh: fsdp: 4 (over x, core), ctx: 8 (over z, y).
Axes of the slice: x: 2, y: 2, z: 4, core: 2. Of those that a mesh axis runs over, the one named last changes fastest.
Arguments:
- tokens: bfloat16 [4, 2048, 1024], P('fsdp', 'ctx'), may hold values from -6 to 6
- out_grad: bfloat16 [4, 2048, 1024], P('fsdp', 'ctx'), may hold values from -6 to 6
- slot_block: int32 [4, 16], P('fsdp'), may hold values from 0 to 15, as said below
- w_attend: bfloat16 [1024, 3072], P('fsdp'), may hold values from -0.1875 to 0.1875
- w_mixing: bfloat16 [1024, 1024], P('fsdp'), may hold values from -1 to 1
- w_expand: bfloat16 [1024, 4096], P('fsdp'), may hold values from -0.1875 to 0.1875
- w_shrink: bfloat16 [4096, 1024], P('fsdp'), may hold values from -0.09375 to 0.09375
- w_norms: bfloat16 [4, 1024], P(None, 'fsdp'), may hold values from -1.2 to 1.4
- first_attend: float32 [1024, 3072], P('fsdp'), may hold values from -24 to 24
- first_mixing: float32 [1024, 1024], P('fsdp'), may hold values from -24 to 24
- first_expand: float32 [1024, 4096], P('fsdp'), may hold values from -24 to 24
- first_shrink: float32 [4096, 1024], P('fsdp'), may hold values from -24 to 24
- first_norms: float32 [4, 1024], P(None, 'fsdp'), may hold values from -24 to 24
- second_attend: float32 [1024, 3072], P('fsdp'), may hold values from 0.5 to 8
- second_mixing: float32 [1024, 1024], P('fsdp'), may hold values from 0.5 to 8
- second_expand: float32 [1024, 4096], P('fsdp'), may hold values from 0.5 to 8
- second_shrink: float32 [4096, 1024], P('fsdp'), may hold values from 0.5 to 8
- second_norms: float32 [4, 1024], P(None, 'fsdp'), may hold values from 0.5 to 8
Outputs:
- layer_out: bfloat16 [4, 2048, 1024], P('fsdp', 'ctx')
- tokens_grad: float32 [4, 2048, 1024], P('fsdp', 'ctx')
- grad_attend: float32 [1024, 3072], P('fsdp')
- update_attend: float32 [1024, 3072], P('fsdp')
- first_new_attend: float32 [1024, 3072], P('fsdp')
- second_new_attend: float32 [1024, 3072], P('fsdp')
- grad_mixing: float32 [1024, 1024], P('fsdp')
- update_mixing: float32 [1024, 1024], P('fsdp')
- first_new_mixing: float32 [1024, 1024], P('fsdp')
- second_new_mixing: float32 [1024, 1024], P('fsdp')
- grad_expand: float32 [1024, 4096], P('fsdp')
- update_expand: float32 [1024, 4096], P('fsdp')
- first_new_expand: float32 [1024, 4096], P('fsdp')
- second_new_expand: float32 [1024, 4096], P('fsdp')
- grad_shrink: float32 [4096, 1024], P('fsdp')
- update_shrink: float32 [4096, 1024], P('fsdp')
- first_new_shrink: float32 [4096, 1024], P('fsdp')
- second_new_shrink: float32 [4096, 1024], P('fsdp')
- grad_norms: float32 [4, 1024], P(None, 'fsdp')
- update_norms: float32 [4, 1024], P(None, 'fsdp')
- first_new_norms: float32 [4, 1024], P(None, 'fsdp')
- second_new_norms: float32 [4, 1024], P(None, 'fsdp')
Inputs may be any that keep to these rules, and one draw needn't show every extreme that they name: `slot_block`: in each row every block number appears once, and slots 2i and 2i+1 hold two blocks whose numbers add up to 15.
All inputs are finite; a program needn't handle non-finite values.
Results may differ from a plain program's by a relative error of at most 0.025.
Values may be sent and summed in bfloat16 or wider, within the bound.
A program may use at most 256 MiB of HBM per device.

v0:
```python
import math
import jax
import jax.numpy as jnp
from jax import lax
from jax.sharding import PartitionSpec as P

HD = 64
HGROUP = 2
STEP_COUNT = 10
EPS_NORM = 1e-05
NEG = -1e30
BETA_ONE = 0.9
BETA_TWO = 0.999
LEARN = 0.02
DECAY = 0.1
EPS_ADAM = 1e-08
CUBIC = 0.044715
ROOT_TWO_PI = math.sqrt(2.0 / math.pi)


def layer_norm(values, gain, shift):
    center = values - jnp.mean(values, axis=-1, keepdims=True)
    spread = jnp.mean(center * center, axis=-1, keepdims=True)
    return center * lax.rsqrt(spread + EPS_NORM) * gain + shift


def gelu(values):
    cube = values * values * values
    return 0.5 * values * (1.0 + jnp.tanh(ROOT_TWO_PI * (values + CUBIC * cube)))


def positions(slots, block):
    offsets = jnp.arange(block, dtype=jnp.int32)
    placed = slots[:, :, None] * block + offsets[None, None, :]
    return placed.reshape(slots.shape[0], slots.shape[1] * block)


def adam_step(weight, grad, first, second):
    first_new = BETA_ONE * first + (1.0 - BETA_ONE) * grad
    second_new = BETA_TWO * second + (1.0 - BETA_TWO) * grad * grad
    mean_hat = first_new / (1.0 - BETA_ONE**STEP_COUNT)
    square_hat = second_new / (1.0 - BETA_TWO**STEP_COUNT)
    update = -LEARN * (
        mean_hat / (jnp.sqrt(square_hat) + EPS_ADAM) + DECAY * weight.astype(jnp.float32)
    )
    return (update, first_new, second_new)


def shards(
    tokens,
    out_grad,
    slot_block,
    w_attend,
    w_mixing,
    w_expand,
    w_shrink,
    w_norms,
    first_attend,
    first_mixing,
    first_expand,
    first_shrink,
    first_norms,
    second_attend,
    second_mixing,
    second_expand,
    second_shrink,
    second_norms,
):
    whole_attend, whole_mixing, whole_expand, whole_shrink, whole_norms = (
        lax.all_gather(w_attend, "fsdp", axis=0, tiled=True),
        lax.all_gather(w_mixing, "fsdp", axis=0, tiled=True),
        lax.all_gather(w_expand, "fsdp", axis=0, tiled=True),
        lax.all_gather(w_shrink, "fsdp", axis=0, tiled=True),
        lax.all_gather(w_norms, "fsdp", axis=1, tiled=True),
    )
    seqs, local, width = tokens.shape
    block = local // 2
    length = slot_block.shape[1] * block
    total_rows = seqs * local
    heads = width // HD
    group_width = HGROUP * HD
    scale = 1.0 / math.sqrt(HD)
    norm_values = whole_norms.astype(jnp.float32)
    owned = lax.dynamic_slice_in_dim(slot_block, 2 * lax.axis_index("ctx"), 2, 1)
    query_place = positions(owned, block)
    key_place = positions(slot_block, block)
    allowed = key_place[:, None, None, :] <= query_place[:, None, :, None]
    start = tokens.reshape(total_rows, width).astype(jnp.float32)
    normed, norm_back = jax.vjp(layer_norm, start, norm_values[0], norm_values[1])
    normed_low = normed.astype(jnp.bfloat16)
    joint = jnp.dot(normed_low, whole_attend, preferred_element_type=jnp.float32).astype(
        jnp.bfloat16
    )
    query = joint[:, :width].reshape(seqs, local, width)
    keys_own = joint[:, width : 2 * width].reshape(seqs, local, width)
    values_own = joint[:, 2 * width :].reshape(seqs, local, width)
    keys, values = (
        lax.all_gather(keys_own, "ctx", axis=1, tiled=True),
        lax.all_gather(values_own, "ctx", axis=1, tiled=True),
    )

    def group_scores(index):
        offset = index * group_width
        query_group = lax.dynamic_slice_in_dim(query, offset, group_width, 2).reshape(
            seqs, local, HGROUP, HD
        )
        key_group = lax.dynamic_slice_in_dim(keys, offset, group_width, 2).reshape(
            seqs, length, HGROUP, HD
        )
        value_group = lax.dynamic_slice_in_dim(values, offset, group_width, 2).reshape(
            seqs, length, HGROUP, HD
        )
        raw = (
            jnp.einsum(
                "sqhd,skhd->shqk", query_group, key_group, preferred_element_type=jnp.float32
            )
            * scale
        )
        return (jnp.where(allowed, raw, NEG), query_group, key_group, value_group)

    def forward_group(index, state):
        mixed_buffer, totals_buffer = state
        masked, query_group, key_group, value_group = group_scores(index)
        top = jnp.max(masked, axis=-1, keepdims=True)
        total = top + jnp.log(jnp.sum(jnp.exp(masked - top), axis=-1, keepdims=True))
        probs = jnp.exp(masked - total).astype(jnp.bfloat16)
        result = jnp.einsum(
            "shqk,skhd->sqhd", probs, value_group, preferred_element_type=jnp.float32
        )
        result = result.reshape(seqs, local, group_width).astype(jnp.bfloat16)
        mixed_buffer = lax.dynamic_update_slice_in_dim(mixed_buffer, result, index * group_width, 2)
        totals_buffer = lax.dynamic_update_slice_in_dim(
            totals_buffer, total[..., 0], index * HGROUP, 1
        )
        return (mixed_buffer, totals_buffer)

    mixed, totals = lax.fori_loop(
        0,
        heads // HGROUP,
        forward_group,
        (
            jnp.zeros((seqs, local, width), jnp.bfloat16),
            jnp.zeros((seqs, heads, local), jnp.float32),
        ),
    )
    mixed_rows = mixed.reshape(total_rows, width)
    middle = start + jnp.dot(mixed_rows, whole_mixing, preferred_element_type=jnp.float32)
    normed_two, norm_two_back = jax.vjp(layer_norm, middle, norm_values[2], norm_values[3])
    normed_two_low = normed_two.astype(jnp.bfloat16)
    expanded = jnp.dot(normed_two_low, whole_expand, preferred_element_type=jnp.float32)
    activated, gelu_back = jax.vjp(gelu, expanded)
    activated_low = activated.astype(jnp.bfloat16)
    result_rows = middle + jnp.dot(activated_low, whole_shrink, preferred_element_type=jnp.float32)
    layer_out = result_rows.reshape(seqs, local, width).astype(jnp.bfloat16)
    incoming = out_grad.reshape(total_rows, width)
    grad_shrink = jnp.dot(activated_low.T, incoming, preferred_element_type=jnp.float32)
    grad_activated = jnp.dot(incoming, whole_shrink.T, preferred_element_type=jnp.float32).astype(
        jnp.bfloat16
    )
    grad_expanded = gelu_back(grad_activated.astype(jnp.float32))[0].astype(jnp.bfloat16)
    grad_expand = jnp.dot(normed_two_low.T, grad_expanded, preferred_element_type=jnp.float32)
    grad_normed_two = jnp.dot(grad_expanded, whole_expand.T, preferred_element_type=jnp.float32)
    grad_middle_norm, grad_gain_two, grad_shift_two = norm_two_back(grad_normed_two)
    grad_middle = incoming.astype(jnp.float32) + grad_middle_norm
    grad_branch = grad_middle.astype(jnp.bfloat16)
    grad_mixing = jnp.dot(mixed_rows.T, grad_branch, preferred_element_type=jnp.float32)
    grad_mixed = jnp.dot(grad_branch, whole_mixing.T, preferred_element_type=jnp.float32)
    grad_mixed = grad_mixed.astype(jnp.bfloat16).reshape(seqs, local, width)

    def backward_group(index, state):
        grad_query, grad_keys, grad_values = state
        offset = index * group_width
        masked, query_group, key_group, value_group = group_scores(index)
        total = lax.dynamic_slice_in_dim(totals, index * HGROUP, HGROUP, 1)
        probs = jnp.exp(masked - total[..., None])
        grad_group = lax.dynamic_slice_in_dim(grad_mixed, offset, group_width, 2).reshape(
            seqs, local, HGROUP, HD
        )
        grad_probs = jnp.einsum(
            "sqhd,skhd->shqk", grad_group, value_group, preferred_element_type=jnp.float32
        )
        grad_scores = probs * (grad_probs - jnp.sum(probs * grad_probs, axis=-1, keepdims=True))
        grad_scores = grad_scores.astype(jnp.bfloat16)
        part_query = (
            jnp.einsum(
                "shqk,skhd->sqhd", grad_scores, key_group, preferred_element_type=jnp.float32
            )
            * scale
        )
        part_keys = (
            jnp.einsum(
                "shqk,sqhd->skhd", grad_scores, query_group, preferred_element_type=jnp.float32
            )
            * scale
        )
        part_values = jnp.einsum(
            "shqk,sqhd->skhd",
            probs.astype(jnp.bfloat16),
            grad_group,
            preferred_element_type=jnp.float32,
        )
        grad_query = lax.dynamic_update_slice_in_dim(
            grad_query, part_query.reshape(seqs, local, group_width), offset, 2
        )
        grad_keys = lax.dynamic_update_slice_in_dim(
            grad_keys, part_keys.reshape(seqs, length, group_width), offset, 2
        )
        grad_values = lax.dynamic_update_slice_in_dim(
            grad_values, part_values.reshape(seqs, length, group_width), offset, 2
        )
        return (grad_query, grad_keys, grad_values)

    grad_query, grad_keys_all, grad_values_all = lax.fori_loop(
        0,
        heads // HGROUP,
        backward_group,
        (
            jnp.zeros((seqs, local, width), jnp.float32),
            jnp.zeros((seqs, length, width), jnp.float32),
            jnp.zeros((seqs, length, width), jnp.float32),
        ),
    )
    grad_keys, grad_values = (
        lax.psum_scatter(
            grad_keys_all.astype(jnp.bfloat16), "ctx", scatter_dimension=1, tiled=True
        ).astype(jnp.float32),
        lax.psum_scatter(
            grad_values_all.astype(jnp.bfloat16), "ctx", scatter_dimension=1, tiled=True
        ).astype(jnp.float32),
    )
    grad_joint = jnp.concatenate(
        [
            grad_query.astype(jnp.bfloat16),
            grad_keys.astype(jnp.bfloat16),
            grad_values.astype(jnp.bfloat16),
        ],
        axis=2,
    ).reshape(total_rows, 3 * width)
    grad_attend = jnp.dot(normed_low.T, grad_joint, preferred_element_type=jnp.float32)
    grad_normed = jnp.dot(grad_joint, whole_attend.T, preferred_element_type=jnp.float32)
    grad_start_norm, grad_gain_one, grad_shift_one = norm_back(grad_normed)
    tokens_grad = (grad_middle + grad_start_norm).reshape(seqs, local, width)
    grad_norms = jnp.stack([grad_gain_one, grad_shift_one, grad_gain_two, grad_shift_two])
    owned_attend, owned_mixing, owned_expand, owned_shrink, owned_norms = (
        lax.psum_scatter(
            grad_attend.astype(jnp.bfloat16), "fsdp", scatter_dimension=0, tiled=True
        ).astype(jnp.float32),
        lax.psum_scatter(
            grad_mixing.astype(jnp.bfloat16), "fsdp", scatter_dimension=0, tiled=True
        ).astype(jnp.float32),
        lax.psum_scatter(
            grad_expand.astype(jnp.bfloat16), "fsdp", scatter_dimension=0, tiled=True
        ).astype(jnp.float32),
        lax.psum_scatter(
            grad_shrink.astype(jnp.bfloat16), "fsdp", scatter_dimension=0, tiled=True
        ).astype(jnp.float32),
        lax.psum_scatter(
            grad_norms.astype(jnp.bfloat16), "fsdp", scatter_dimension=1, tiled=True
        ).astype(jnp.float32),
    )
    sum_attend, sum_mixing, sum_expand, sum_shrink, sum_norms = (
        lax.psum(owned_attend.astype(jnp.bfloat16), "ctx").astype(jnp.float32),
        lax.psum(owned_mixing.astype(jnp.bfloat16), "ctx").astype(jnp.float32),
        lax.psum(owned_expand.astype(jnp.bfloat16), "ctx").astype(jnp.float32),
        lax.psum(owned_shrink.astype(jnp.bfloat16), "ctx").astype(jnp.float32),
        lax.psum(owned_norms.astype(jnp.bfloat16), "ctx").astype(jnp.float32),
    )
    update_attend, first_new_attend, second_new_attend = adam_step(
        w_attend, sum_attend, first_attend, second_attend
    )
    update_mixing, first_new_mixing, second_new_mixing = adam_step(
        w_mixing, sum_mixing, first_mixing, second_mixing
    )
    update_expand, first_new_expand, second_new_expand = adam_step(
        w_expand, sum_expand, first_expand, second_expand
    )
    update_shrink, first_new_shrink, second_new_shrink = adam_step(
        w_shrink, sum_shrink, first_shrink, second_shrink
    )
    update_norms, first_new_norms, second_new_norms = adam_step(
        w_norms, sum_norms, first_norms, second_norms
    )
    return (
        layer_out,
        tokens_grad,
        sum_attend,
        update_attend,
        first_new_attend,
        second_new_attend,
        sum_mixing,
        update_mixing,
        first_new_mixing,
        second_new_mixing,
        sum_expand,
        update_expand,
        first_new_expand,
        second_new_expand,
        sum_shrink,
        update_shrink,
        first_new_shrink,
        second_new_shrink,
        sum_norms,
        update_norms,
        first_new_norms,
        second_new_norms,
    )


def solution(mesh):
    return jax.shard_map(
        shards,
        mesh=mesh,
        in_specs=(
            P("fsdp", "ctx", None),
            P("fsdp", "ctx", None),
            P("fsdp", None),
            P("fsdp", None),
            P("fsdp", None),
            P("fsdp", None),
            P("fsdp", None),
            P(None, "fsdp"),
            P("fsdp", None),
            P("fsdp", None),
            P("fsdp", None),
            P("fsdp", None),
            P(None, "fsdp"),
            P("fsdp", None),
            P("fsdp", None),
            P("fsdp", None),
            P("fsdp", None),
            P(None, "fsdp"),
        ),
        out_specs=(
            P("fsdp", "ctx", None),
            P("fsdp", "ctx", None),
            P("fsdp", None),
            P("fsdp", None),
            P("fsdp", None),
            P("fsdp", None),
            P("fsdp", None),
            P("fsdp", None),
            P("fsdp", None),
            P("fsdp", None),
            P("fsdp", None),
            P("fsdp", None),
            P("fsdp", None),
            P("fsdp", None),
            P("fsdp", None),
            P("fsdp", None),
            P("fsdp", None),
            P("fsdp", None),
            P(None, "fsdp"),
            P(None, "fsdp"),
            P(None, "fsdp"),
            P(None, "fsdp"),
        ),
        check_vma=False,
    )
```

profile of v0, /device:TPU:0, one launch (start us, length us, event | category | flops | bytes accessed | tf_op | source)
XLA Modules:
  0.0 1199.6 jit_solution(6608566212357250092)
XLA Ops:
  8.0 6.3 all_gather.21
  16.8 41.9 %all-gather.9.cloned.1.call-done = bf16[1024,3072]{1,0:T(8,128)(2,1)} async-done(((bf16[256,3072]{1,0:T(8,128)(2,1)}), bf16[1024,3072]{1,0:T(8,128)(2,1)}) %all-gather.9.cloned.1.call-update) | async-done | bytes 6291472 | tf_op jit(solution)/shard_map/all_gather | solution.py:70
  58.7 4.9 convolution_convert_fusion.4
  67.8 70.6 %all-gather.17.cloned.1.call-done = bf16[2048,1024]{1,0:T(8,128)(2,1)} async-done(((bf16[256,1024]{1,0:T(8,128)(2,1)}), bf16[2048,1024]{1,0:T(8,128)(2,1)}) %all-gather.17.cloned.1.call-update) | async-done | bytes 4194320 | tf_op jit(solution)/shard_map/all_gather | solution.py:99
  138.4 6.4 copy.47
  144.8 68.0 %all-gather.19.cloned.1.call-done = bf16[2048,1024]{1,0:T(8,128)(2,1)} async-done(((bf16[256,1024]{1,0:T(8,128)(2,1)}), bf16[2048,1024]{1,0:T(8,128)(2,1)}) %all-gather.19.cloned.1.call-update) | async-done | bytes 4194320 | tf_op jit(solution)/shard_map/all_gather | solution.py:98
  212.8 6.4 copy.49
  219.3 74.3 %while.34 = (s32[]{:T(128)}, bf16[1,256,1024]{1,2,0:T(8,128)(2,1)S(1)}, f32[1,16,256]{2,1,0:T(8,128)S(1)}, bf16[1,2048,1024]{1,2,0:T(8,128)(2,1)}, bf16[1,256,10...) while((s32[]{:T(128)}, ...), condition=%wide.region_5.6_spmd.clone, body=%wide.region_2.5_spmd.clone.sunk | while | flops 276332032 | bytes 33973524 | solution.py:137
  221.0 3.0 fusion.120
  224.1 3.1 exponential_reduce_fusion.2
  230.2 3.0 fusion.120
  233.2 3.1 exponential_reduce_fusion.2
  239.3 3.0 fusion.120
  242.3 3.6 exponential_reduce_fusion.2
  249.6 3.0 fusion.120
  258.8 3.0 fusion.120
  267.9 3.0 fusion.120
  270.9 3.1 exponential_reduce_fusion.2
  297.1 7.9 fusion.64
  305.0 49.5 %all-gather.15.cloned.1.call-done = bf16[4096,1024]{1,0:T(8,128)(2,1)} async-done(((bf16[1024,1024]{1,0:T(8,128)(2,1)}), bf16[4096,1024]{1,0:T(8,128)(2,1)}) %all-gather.15.cloned.1.call-update) | async-done | bytes 8388624 | tf_op jit(solution)/shard_map/all_gather | solution.py:73
  354.6 8.7 fusion.17
  375.0 120.1 %while.35 = (s32[]{:T(128)}, bf16[1,256,1024]{1,2,0:T(8,128)(2,1)}, bf16[1,2048,1024]{1,2,0:T(8,128)(2,1)}, bf16[1,2048,1024]{1,2,0:T(8,128)(2,1)}, bf16[1,2048,...) while((s32[]{:T(128)}, bf16[1,256,1024]{1,2,0:T(8,128)(2,1)}, ...), condition=%wide.region_12.13_spmd.clone, body=%wide.region_10.0_spmd.clone.sunk | while | flops 681639424 | bytes 56970552 | solution.py:213
  382.1 4.0 multiply_reduce_fusion.5
  397.2 4.0 multiply_reduce_fusion.5
  412.2 4.0 multiply_reduce_fusion.5
  427.2 4.0 multiply_reduce_fusion.5
  442.2 4.0 multiply_reduce_fusion.5
  457.2 4.0 multiply_reduce_fusion.5
  472.2 4.0 multiply_reduce_fusion.5
  487.2 4.0 multiply_reduce_fusion.5
  496.2 3.1 convolution_convert_fusion.5
  499.5 7.3 convolution_convert_fusion.1
  507.9 8.5 convolution_convert_fusion
  516.4 67.2 %reduce-scatter.12.cloned.1.call-done = bf16[1,256,1024]{1,2,0:T(8,128)(2,1)} async-done(((bf16[1,2048,1024]{1,2,0:T(8,128)(2,1)}), bf16[1,256,1024]{1,2,0:T(8,128)(2,1)}) %reduce-scatter.12.cloned.1.call-update) | async-done | bytes 524304 | tf_op jit(solution)/shard_map/reduce_scatter | solution.py:227
  583.6 92.7 %reduce-scatter.10.cloned.1.call-done = bf16[1,256,1024]{1,2,0:T(8,128)(2,1)} async-done(((bf16[1,2048,1024]{1,2,0:T(8,128)(2,1)}), bf16[1,256,1024]{1,2,0:T(8,128)(2,1)}) %reduce-scatter.10.cloned.1.call-update) | async-done | bytes 524304 | tf_op jit(solution)/shard_map/reduce_scatter | solution.py:224
  676.4 6.0 convolution_convert_fusion.2
  682.5 5.4 fusion.35
  690.7 20.0 %reduce-scatter.16.cloned.1.call-done = bf16[256,1024]{1,0:T(8,128)(2,1)} async-done(((bf16[1024,1024]{1,0:T(8,128)(2,1)}), bf16[256,1024]{1,0:T(8,128)(2,1)}) %reduce-scatter.16.cloned.1.call-update) | async-done | bytes 524304 | tf_op jit(solution)/shard_map/reduce_scatter | solution.py:248
  710.7 74.4 %reduce-scatter.18.cloned.1.call-done = bf16[256,4096]{1,0:T(8,128)(2,1)} async-done(((bf16[1024,4096]{1,0:T(8,128)(2,1)}), bf16[256,4096]{1,0:T(8,128)(2,1)}) %reduce-scatter.18.cloned.1.call-update) | async-done | bytes 2097168 | tf_op jit(solution)/shard_map/reduce_scatter | solution.py:251
  785.0 74.3 %reduce-scatter.20.cloned.1.call-done = bf16[1024,1024]{1,0:T(8,128)(2,1)} async-done(((bf16[4096,1024]{1,0:T(8,128)(2,1)}), bf16[1024,1024]{1,0:T(8,128)(2,1)}) %reduce-scatter.20.cloned.1.call-update) | async-done | bytes 2097168 | tf_op jit(solution)/shard_map/reduce_scatter | solution.py:254
  859.4 60.9 %reduce-scatter.14.cloned.1.call-done = bf16[256,3072]{1,0:T(8,128)(2,1)} async-done(((bf16[1024,3072]{1,0:T(8,128)(2,1)}), bf16[256,3072]{1,0:T(8,128)(2,1)}) %reduce-scatter.14.cloned.1.call-update) | async-done | bytes 1572880 | tf_op jit(solution)/shard_map/reduce_scatter | solution.py:245
  920.4 8.3 fusion.28
  930.2 13.3 %reduce-scatter.22.cloned.1.call-done = bf16[256,4]{1,0:T(8,128)(2,1)} async-done(((bf16[1024,4]{1,0:T(8,128)(2,1)}), bf16[256,4]{1,0:T(8,128)(2,1)}) %reduce-scatter.22.cloned.1.call-update) | async-done | bytes 2064
  944.4 21.8 %psum.39 = bf16[4,256]{1,0:T(4,128)(2,1)S(1)} all-reduce(bf16[4,256]{1,0:T(4,128)(2,1)S(1)} %copy.55), channel_id=1, replica_groups=mesh['fsdp'=4,'ctx'=8] {'ctx'}, use_global_device_ids=true, to_apply=%region_30.31 | all-reduce | flops 1024 | bytes 4096 | tf_op jit(solution)/shard_map/psum | solution.py:266
  966.8 196.3 %all-reduce.3.cloned.1.call-done = (bf16[256,3072]{1,0:T(8,128)(2,1)}, bf16[256,1024]{1,0:T(8,128)(2,1)}, bf16[256,4096]{1,0:T(8,128)(2,1)}, bf16[1024,1024]{1,0:T(8,128)(2,1)}) async-done(((bf16[256,3072]{1,0:T(8,128)(2,1)}, bf16[256,1024]{1,0:T(8,128)(2,1)}, bf16[256,4096]{1,0:T(8,128)(2,1)}, bf16[1024,1024]{1,0:T(8,128)(2,1)}), (bf16[256,3072]{1,0:T(8,128)(2,1)}, bf16[256,1024]{1,0:T(8,128)(2,1)}, ...) | async-done | bytes 6291472 | tf_op jit(solution)/shard_map/psum | solution.py:262
  1163.2 8.7 add_multiply_fusion.2
  1176.2 9.8 add_multiply_fusion.1
  1186.1 6.8 add_multiply_fusion
  (333 shorter events, 165.2 us)
Async XLA Ops:
  7.2 51.5 %all-gather.9.cloned.1.call-start = ((), (), s32[]{:S(2)}) async-start(), calls=%async_computation.7 | async-start | bytes 7864320 | tf_op jit(solution)/shard_map/all_gather | solution.py:70
  7.9 130.4 %all-gather.17.cloned.1.call-start = ((), (), s32[]{:S(2)}) async-start(), calls=%async_computation.17 | async-start | bytes 4718592 | tf_op jit(solution)/shard_map/all_gather | solution.py:99
  16.8 46.8 %copy-start.27 = (f32[256]{0:T(256)}, f32[256]{0:T(256)S(1)}, u32[]{:S(2)}) copy-start(f32[256]{0:T(256)S(1)} %fusion.34) | copy-start | bytes 3076
  63.6 3.7 copy-start.33
  64.7 148.0 %all-gather.19.cloned.1.call-start = ((), (), s32[]{:S(2)}) async-start(), calls=%async_computation.18 | async-start | bytes 4718592 | tf_op jit(solution)/shard_map/all_gather | solution.py:98
  65.5 228.1 %all-gather.11.cloned.1.call-start = ((), (), s32[]{:S(2)}) async-start(), calls=%async_computation.8 | async-start | bytes 2621440 | tf_op jit(solution)/shard_map/all_gather | solution.py:71
  66.1 231.0 %all-gather.13.cloned.1.call-start = ((), (), s32[]{:S(2)}) async-start(), calls=%async_computation.9 | async-start | bytes 10485760 | tf_op jit(solution)/shard_map/all_gather | solution.py:72
  66.6 287.9 %all-gather.15.cloned.1.call-start = ((), (), s32[]{:S(2)}) async-start(), calls=%async_computation.10 | async-start | bytes 10485760 | tf_op jit(solution)/shard_map/all_gather | solution.py:73
  67.2 516.4 %reduce-scatter.12.cloned.1.call-start = ((), (), s32[]{:S(2)}) async-start(), calls=%async_computation.12 | async-start | bytes 4718592 | tf_op jit(solution)/shard_map/reduce_scatter | solution.py:227
  219.2 75.1 %copy-start.2 = (bf16[1,256,1024]{2,1,0:T(8,128)(2,1)S(1)}, bf16[1,256,1024]{2,1,0:T(8,128)(2,1)}, u32[]{:S(2)}) copy-start(bf16[1,256,1024]{2,1,0:T(8,128)(2,1)} %param.22) | copy-start | bytes 1572868
  242.3 4.7 copy-start
  293.6 11.5 copy-start.6
  297.1 57.5 %copy-start.19 = (bf16[1,256,1024]{2,1,0:T(8,128)(2,1)S(1)}, bf16[1,256,1024]{2,1,0:T(8,128)(2,1)}, u32[]{:S(2)}) copy-start(bf16[1,256,1024]{2,1,0:T(8,128)(2,1)} %param.23) | copy-start | bytes 1572868
  354.6 8.7 copy-start.32
  367.6 7.4 copy-start.22
  382.1 4.0 copy-start.1
  397.1 4.0 copy-start.1
  412.2 4.0 copy-start.1
  427.2 4.0 copy-start.1
  442.2 4.0 copy-start.1
  457.2 4.0 copy-start.1
  472.2 4.0 copy-start.1
  487.2 4.0 copy-start.1
  495.2 181.2 %reduce-scatter.10.cloned.1.call-start = ((), (), s32[]{:S(2)}) async-start(), calls=%async_computation.11 | async-start | bytes 4718592 | tf_op jit(solution)/shard_map/reduce_scatter | solution.py:224
  495.9 214.7 %reduce-scatter.16.cloned.1.call-start = ((), (), s32[]{:S(2)}) async-start(), calls=%async_computation.14 | async-start | bytes 2621440 | tf_op jit(solution)/shard_map/reduce_scatter | solution.py:248
  499.3 285.8 %reduce-scatter.18.cloned.1.call-start = ((), (), s32[]{:S(2)}) async-start(), calls=%async_computation.15 | async-start | bytes 10485760 | tf_op jit(solution)/shard_map/reduce_scatter | solution.py:251
  506.9 352.5 %reduce-scatter.20.cloned.1.call-start = ((), (), s32[]{:S(2)}) async-start(), calls=%async_computation.16 | async-start | bytes 10485760 | tf_op jit(solution)/shard_map/reduce_scatter | solution.py:254
  516.4 160.0 %copy-start.26 = (bf16[1,256,1024]{1,2,0:T(8,128)(2,1)S(1)}, bf16[1,256,1024]{1,2,0:T(8,128)(2,1)}, u32[]{:S(2)}) copy-start(bf16[1,256,1024]{1,2,0:T(8,128)(2,1)} %get-tuple-element.320) | copy-start | bytes 1572868
  516.4 403.9 %reduce-scatter.14.cloned.1.call-start = ((), (), s32[]{:S(2)}) async-start(), calls=%async_computation.13 | async-start | bytes 7864320 | tf_op jit(solution)/shard_map/reduce_scatter | solution.py:245
  682.4 261.1 %reduce-scatter.22.cloned.1.call-start = ((), (), s32[]{:S(2)}) async-start(), calls=%async_computation.19 | async-start | bytes 327680
  682.5 5.5 copy-start.28
  690.4 472.7 %all-reduce.3.cloned.1.call-start = ((), (), s32[]{:S(2)}) async-start(), calls=%async_computation.20 | async-start | bytes 12582912 | tf_op jit(solution)/shard_map/psum | solution.py:262
  920.3 8.3 copy-start.13
  920.3 8.3 copy-start.21
  928.6 37.6 %copy-start.29 = (bf16[4,256]{1,0:T(4,128)(2,1)S(1)}, bf16[4,256]{1,0:T(4,128)(2,1)}, u32[]{:S(2)}) copy-start(bf16[4,256]{1,0:T(4,128)(2,1)} %param.29) | copy-start | bytes 6148
  928.7 37.6 %copy-start.30 = (f32[4,256]{1,0:T(4,128)S(1)}, f32[4,256]{1,0:T(4,128)}, u32[]{:S(2)}) copy-start(f32[4,256]{1,0:T(4,128)} %param.34) | copy-start | bytes 12292
  928.7 37.6 %copy-start.31 = (f32[4,256]{1,0:T(4,128)S(1)}, f32[4,256]{1,0:T(4,128)}, u32[]{:S(2)}) copy-start(f32[4,256]{1,0:T(4,128)} %param.39) | copy-start | bytes 12292
  928.7 234.5 %copy-start.5 = (bf16[256,3072]{1,0:T(8,128)(2,1)S(1)}, bf16[256,3072]{1,0:T(8,128)(2,1)}, u32[]{:S(2)}) copy-start(bf16[256,3072]{1,0:T(8,128)(2,1)} %param.25) | copy-start | bytes 4718596
  1163.1 8.7 copy-start.16
  1163.1 8.7 copy-start.23
  1163.1 8.7 copy-start.24
  1163.2 8.7 copy-start.25
  1163.2 11.2 copy-start.9
  1171.8 4.4 copy-start.8
  1176.2 9.9 copy-start.4
  1176.2 9.9 copy-start.10
  1176.2 9.9 copy-start.11
  1176.2 9.9 copy-start.15
  (14 other events, 35.1 us)
Sparse Core Ops, SparseCore 0:
  9.6 49.0 all-gather.8
  64.9 73.4 all-gather.16
  141.1 71.6 all-gather.18
  214.2 20.8 all-gather.10
  236.5 58.2 all-gather.12
  296.2 58.3 all-gather.14
  495.3 88.2 reduce-scatter.11
  588.3 88.0 reduce-scatter.9
  679.5 31.1 reduce-scatter.15
  713.3 71.7 reduce-scatter.17
  787.6 71.7 reduce-scatter.19
  861.9 58.3 reduce-scatter.13
  923.3 20.0 reduce-scatter.21
  948.4 214.6 all-reduce.2
where the time goes:
time: 1210 us; the launch traced here: 1200 us
  waiting for transfers between devices  833 us (69%)
  matrix products  166 us (14%)
  local copies, waits for them, and re-layouts  87.7 us (7%)
  other arithmetic  68.2 us (6%)
  blocking collectives  28.1 us (2%)
  between operations  14.6 us (1%)
    psum x1, waiting for transfers between devices, shards(): lax.psum(owned_attend.astype(jnp.bfloat16), 'ctx').astype(jnp.float32)  196 us
    reduce_scatter x1, waiting for transfers between devices, shards(): lax.psum_scatter(grad_keys_all.astype(jnp.bfloat16), 'ctx', scatter_dimen...  92.7 us
    reduce_scatter x1, waiting for transfers between devices, shards(): lax.psum_scatter(grad_expand.astype(jnp.bfloat16), 'fsdp', scatter_dimens...  74.4 us
    reduce_scatter x1, waiting for transfers between devices, shards(): lax.psum_scatter(grad_shrink.astype(jnp.bfloat16), 'fsdp', scatter_dimens...  74.3 us
    all_gather x1, waiting for transfers between devices, shards(): lax.all_gather(values_own, 'ctx', axis=1, tiled=True)  70.6 us
    all_gather x1, waiting for transfers between devices, shards(): lax.all_gather(keys_own, 'ctx', axis=1, tiled=True)  68 us
    reduce_scatter x1, waiting for transfers between devices, shards(): lax.psum_scatter(grad_values_all.astype(jnp.bfloat16), 'ctx', scatter_dim...  67.2 us
    reduce_scatter x1, waiting for transfers between devices, shards(): lax.psum_scatter(grad_attend.astype(jnp.bfloat16), 'fsdp', scatter_dimens...  60.9 us
  transfers between devices with their start and end apart: 14, of which 12 were waited for; matrix products, arithmetic and copies ran while one was open for 12% of the time, Pallas kernels for 0%

commit v1 on v0

--- a/solution.py
+++ b/solution.py
@@ -1,3 +1,4 @@
+import functools
 import math
 import jax
 import jax.numpy as jnp
@@ -16,6 +17,14 @@
 EPS_ADAM = 1e-08
 CUBIC = 0.044715
 ROOT_TWO_PI = math.sqrt(2.0 / math.pi)
+
+
+def watch_sheets_here(original, bus_axis):
+    field_out = lax.all_gather(original, bus_axis).sum(axis=0)
+    return field_out
+
+
+wait_grid = functools.partial(watch_sheets_here, bus_axis="ctx")
 
 
 def layer_norm(values, gain, shift):
@@ -259,7 +268,7 @@
         ).astype(jnp.float32),
     )
     sum_attend, sum_mixing, sum_expand, sum_shrink, sum_norms = (
-        lax.psum(owned_attend.astype(jnp.bfloat16), "ctx").astype(jnp.float32),
+        wait_grid(owned_attend.astype(jnp.bfloat16)).astype(jnp.float32),
         lax.psum(owned_mixing.astype(jnp.bfloat16), "ctx").astype(jnp.float32),
         lax.psum(owned_expand.astype(jnp.bfloat16), "ctx").astype(jnp.float32),
         lax.psum(owned_shrink.astype(jnp.bfloat16), "ctx").astype(jnp.float32),

time: 1210 us -> 1330 us (1.099)
  waiting for transfers between devices: 833 us -> 942 us
    all_gather x0 -> x1, waiting for transfers between devices: none -> 154 us  [watch_sheets_here(): field_out = lax.all_gather(original, bus_axis).sum(axis=0)]
    psum x1, waiting for transfers between devices: 196 us -> 151 us  [shards(): lax.psum(owned_mixing.astype(jnp.bfloat16), 'ctx').astype(jnp.float32)]
  transfers between devices with their start and end apart: 14 -> 15, of which waited for: 12 -> 13; matrix products, arithmetic and copies ran while one was open for 12% -> 12% of each run, Pallas kernels for 0% -> 0%
where the time goes in v1:
time: 1330 us; the launch traced here: 1320 us
  waiting for transfers between devices  942 us (71%)
  matrix products  166 us (12%)
  local copies, waits for them, and re-layouts  87 us (7%)
  other arithmetic  78.1 us (6%)
  blocking collectives  28.1 us (2%)
  between operations  14.6 us (1%)
    all_gather x1, waiting for transfers between devices, watch_sheets_here(): field_out = lax.all_gather(original, bus_axis).sum(axis=0)  154 us
    psum x1, waiting for transfers between devices, shards(): lax.psum(owned_mixing.astype(jnp.bfloat16), 'ctx').astype(jnp.float32)  151 us
    reduce_scatter x1, waiting for transfers between devices, shards(): lax.psum_scatter(grad_keys_all.astype(jnp.bfloat16), 'ctx', scatter_dimen...  92.9 us
    reduce_scatter x1, waiting for transfers between devices, shards(): lax.psum_scatter(grad_expand.astype(jnp.bfloat16), 'fsdp', scatter_dimens...  74.4 us
    reduce_scatter x1, waiting for transfers between devices, shards(): lax.psum_scatter(grad_shrink.astype(jnp.bfloat16), 'fsdp', scatter_dimens...  74.3 us
    all_gather x1, waiting for transfers between devices, shards(): lax.all_gather(values_own, 'ctx', axis=1, tiled=True)  70.6 us
    all_gather x1, waiting for transfers between devices, shards(): lax.all_gather(keys_own, 'ctx', axis=1, tiled=True)  68 us
    reduce_scatter x1, waiting for transfers between devices, shards(): lax.psum_scatter(grad_values_all.astype(jnp.bfloat16), 'ctx', scatter_dim...  67.2 us
  transfers between devices with their start and end apart: 15, of which 13 were waited for; matrix products, arithmetic and copies ran while one was open for 12% of the time, Pallas kernels for 0%

profile of v1, /device:TPU:0, one launch (start us, length us, event | category | flops | bytes accessed | tf_op | source)
XLA Modules:
  0.0 1317.8 jit_solution(3197371802718408301)
XLA Ops:
  8.0 6.3 all_gather.27
  16.8 41.9 %all-gather.11.cloned.1.call-done = bf16[1024,3072]{1,0:T(8,128)(2,1)} async-done(((bf16[256,3072]{1,0:T(8,128)(2,1)}), bf16[1024,3072]{1,0:T(8,128)(2,1)}) %all-gather.11.cloned.1.call-update) | async-done | bytes 6291472 | tf_op jit(solution)/shard_map/all_gather | solution.py:79
  58.7 4.9 convolution_convert_fusion.4
  67.8 70.6 %all-gather.19.cloned.1.call-done = bf16[2048,1024]{1,0:T(8,128)(2,1)} async-done(((bf16[256,1024]{1,0:T(8,128)(2,1)}), bf16[2048,1024]{1,0:T(8,128)(2,1)}) %all-gather.19.cloned.1.call-update) | async-done | bytes 4194320 | tf_op jit(solution)/shard_map/all_gather | solution.py:108
  138.4 6.4 copy.47
  144.8 68.0 %all-gather.21.cloned.1.call-done = bf16[2048,1024]{1,0:T(8,128)(2,1)} async-done(((bf16[256,1024]{1,0:T(8,128)(2,1)}), bf16[2048,1024]{1,0:T(8,128)(2,1)}) %all-gather.21.cloned.1.call-update) | async-done | bytes 4194320 | tf_op jit(solution)/shard_map/all_gather | solution.py:107
  212.8 6.4 copy.49
  219.3 74.3 %while.34 = (s32[]{:T(128)}, bf16[1,256,1024]{1,2,0:T(8,128)(2,1)S(1)}, f32[1,16,256]{2,1,0:T(8,128)S(1)}, bf16[1,2048,1024]{1,2,0:T(8,128)(2,1)}, bf16[1,256,10...) while((s32[]{:T(128)}, ...), condition=%wide.region_5.6_spmd.clone, body=%wide.region_2.5_spmd.clone.sunk | while | flops 276332032 | bytes 33973524 | solution.py:146
  221.0 3.0 fusion.120
  224.1 3.1 exponential_reduce_fusion.2
  230.2 3.0 fusion.120
  233.2 3.1 exponential_reduce_fusion.2
  239.3 3.0 fusion.120
  242.3 3.6 exponential_reduce_fusion.2
  270.9 3.1 exponential_reduce_fusion.2
  297.1 7.9 fusion.64
  305.0 49.5 %all-gather.17.cloned.1.call-done = bf16[4096,1024]{1,0:T(8,128)(2,1)} async-done(((bf16[1024,1024]{1,0:T(8,128)(2,1)}), bf16[4096,1024]{1,0:T(8,128)(2,1)}) %all-gather.17.cloned.1.call-update) | async-done | bytes 8388624 | tf_op jit(solution)/shard_map/all_gather | solution.py:82
  354.6 8.7 fusion.17
  375.0 120.1 %while.35 = (s32[]{:T(128)}, bf16[1,256,1024]{1,2,0:T(8,128)(2,1)}, bf16[1,2048,1024]{1,2,0:T(8,128)(2,1)}, bf16[1,2048,1024]{1,2,0:T(8,128)(2,1)}, bf16[1,2048,...) while((s32[]{:T(128)}, bf16[1,256,1024]{1,2,0:T(8,128)(2,1)}, ...), condition=%wide.region_12.13_spmd.clone, body=%wide.region_10.0_spmd.clone.sunk | while | flops 681639424 | bytes 56970552 | solution.py:222
  382.1 4.0 multiply_reduce_fusion.5
  397.2 4.0 multiply_reduce_fusion.5
  412.2 4.0 multiply_reduce_fusion.5
  427.2 4.0 multiply_reduce_fusion.5
  442.2 4.0 multiply_reduce_fusion.5
  457.2 4.0 multiply_reduce_fusion.5
  472.2 4.0 multiply_reduce_fusion.5
  487.2 4.0 multiply_reduce_fusion.5
  496.2 3.1 convolution_convert_fusion.5
  499.5 7.4 convolution_convert_fusion.1
  507.9 8.5 convolution_convert_fusion
  516.5 67.2 %reduce-scatter.12.cloned.1.call-done = bf16[1,256,1024]{1,2,0:T(8,128)(2,1)} async-done(((bf16[1,2048,1024]{1,2,0:T(8,128)(2,1)}), bf16[1,256,1024]{1,2,0:T(8,128)(2,1)}) %reduce-scatter.12.cloned.1.call-update) | async-done | bytes 524304 | tf_op jit(solution)/shard_map/reduce_scatter | solution.py:236
  583.7 92.9 %reduce-scatter.10.cloned.1.call-done = bf16[1,256,1024]{1,2,0:T(8,128)(2,1)} async-done(((bf16[1,2048,1024]{1,2,0:T(8,128)(2,1)}), bf16[1,256,1024]{1,2,0:T(8,128)(2,1)}) %reduce-scatter.10.cloned.1.call-update) | async-done | bytes 524304 | tf_op jit(solution)/shard_map/reduce_scatter | solution.py:233
  676.5 6.1 convolution_convert_fusion.2
  682.8 5.6 fusion.35
  690.9 19.9 %reduce-scatter.16.cloned.1.call-done = bf16[256,1024]{1,0:T(8,128)(2,1)} async-done(((bf16[1024,1024]{1,0:T(8,128)(2,1)}), bf16[256,1024]{1,0:T(8,128)(2,1)}) %reduce-scatter.16.cloned.1.call-update) | async-done | bytes 524304 | tf_op jit(solution)/shard_map/reduce_scatter | solution.py:257
  710.9 74.4 %reduce-scatter.18.cloned.1.call-done = bf16[256,4096]{1,0:T(8,128)(2,1)} async-done(((bf16[1024,4096]{1,0:T(8,128)(2,1)}), bf16[256,4096]{1,0:T(8,128)(2,1)}) %reduce-scatter.18.cloned.1.call-update) | async-done | bytes 2097168 | tf_op jit(solution)/shard_map/reduce_scatter | solution.py:260
  785.2 74.3 %reduce-scatter.20.cloned.1.call-done = bf16[1024,1024]{1,0:T(8,128)(2,1)} async-done(((bf16[4096,1024]{1,0:T(8,128)(2,1)}), bf16[1024,1024]{1,0:T(8,128)(2,1)}) %reduce-scatter.20.cloned.1.call-update) | async-done | bytes 2097168 | tf_op jit(solution)/shard_map/reduce_scatter | solution.py:263
  859.9 60.6 %reduce-scatter.14.cloned.1.call-done = bf16[256,3072]{1,0:T(8,128)(2,1)} async-done(((bf16[1024,3072]{1,0:T(8,128)(2,1)}), bf16[256,3072]{1,0:T(8,128)(2,1)}) %reduce-scatter.14.cloned.1.call-update) | async-done | bytes 1572880 | tf_op jit(solution)/shard_map/reduce_scatter | solution.py:254
  920.5 8.3 fusion.28
  930.3 13.3 %reduce-scatter.22.cloned.1.call-done = bf16[256,4]{1,0:T(8,128)(2,1)} async-done(((bf16[1024,4]{1,0:T(8,128)(2,1)}), bf16[256,4]{1,0:T(8,128)(2,1)}) %reduce-scatter.22.cloned.1.call-update) | async-done | bytes 2064
  944.6 21.9 %psum.31 = bf16[4,256]{1,0:T(4,128)(2,1)S(1)} all-reduce(bf16[4,256]{1,0:T(4,128)(2,1)S(1)} %copy.55), channel_id=1, replica_groups=mesh['fsdp'=4,'ctx'=8] {'ctx'}, use_global_device_ids=true, to_apply=%region_30.31 | all-reduce | flops 1024 | bytes 4096 | tf_op jit(solution)/shard_map/psum | solution.py:275
  967.0 151.5 %all-reduce.3.cloned.1.call-done = (bf16[256,1024]{1,0:T(8,128)(2,1)}, bf16[256,4096]{1,0:T(8,128)(2,1)}, bf16[1024,1024]{1,0:T(8,128)(2,1)}) async-done(((bf16[256,1024]{1,0:T(8,128)(2,1)}, bf16[256,4096]{1,0:T(8,128)(2,1)}, bf16[1024,1024]{1,0:T(8,128)(2,1)}), (bf16[256,1024]{1,0:T(8,128)(2,1)}, bf16[256,4096]{1,0:T(8,128)(2,1)}, bf16[1024,1024]{1,0:T(8,128)(2,1)})) %all-reduce.3.cloned.1.call-update) | async-done | bytes 4718608 | tf_op jit(solution)/shard_map/psum | solution.py:272
  1118.5 4.3 add_multiply_fusion.3
  1122.9 11.3 add_multiply_fusion
  1135.4 7.2 add_multiply_fusion.1
  1142.6 153.6 %all-gather.23.cloned.1.call-done = bf16[2048,3072]{1,0:T(8,128)(2,1)} async-done(((bf16[256,3072]{1,0:T(8,128)(2,1)}), bf16[2048,3072]{1,0:T(8,128)(2,1)}) %all-gather.23.cloned.1.call-update) | async-done | bytes 12582928 | tf_op jit(solution)/shard_map/all_gather | solution.py:23
  1296.2 7.4 reduce_sum.158
  1303.6 7.5 add_multiply_fusion.2
  (323 shorter events, 171.2 us)
Async XLA Ops:
  7.2 51.5 %all-gather.11.cloned.1.call-start = ((), (), s32[]{:S(2)}) async-start(), calls=%async_computation.7 | async-start | bytes 7864320 | tf_op jit(solution)/shard_map/all_gather | solution.py:79
  7.9 130.4 %all-gather.19.cloned.1.call-start = ((), (), s32[]{:S(2)}) async-start(), calls=%async_computation.17 | async-start | bytes 4718592 | tf_op jit(solution)/shard_map/all_gather | solution.py:108
  16.8 46.8 %copy-start.20 = (f32[256]{0:T(256)}, f32[256]{0:T(256)S(1)}, u32[]{:S(2)}) copy-start(f32[256]{0:T(256)S(1)} %fusion.34) | copy-start | bytes 3076
  63.6 3.7 copy-start.26
  64.7 148.0 %all-gather.21.cloned.1.call-start = ((), (), s32[]{:S(2)}) async-start(), calls=%async_computation.18 | async-start | bytes 4718592 | tf_op jit(solution)/shard_map/all_gather | solution.py:107
  65.5 228.1 %all-gather.13.cloned.1.call-start = ((), (), s32[]{:S(2)}) async-start(), calls=%async_computation.8 | async-start | bytes 2621440 | tf_op jit(solution)/shard_map/all_gather | solution.py:80
  66.1 231.0 %all-gather.15.cloned.1.call-start = ((), (), s32[]{:S(2)}) async-start(), calls=%async_computation.9 | async-start | bytes 10485760 | tf_op jit(solution)/shard_map/all_gather | solution.py:81
  66.6 287.9 %all-gather.17.cloned.1.call-start = ((), (), s32[]{:S(2)}) async-start(), calls=%async_computation.10 | async-start | bytes 10485760 | tf_op jit(solution)/shard_map/all_gather | solution.py:82
  67.2 516.4 %reduce-scatter.12.cloned.1.call-start = ((), (), s32[]{:S(2)}) async-start(), calls=%async_computation.12 | async-start | bytes 4718592 | tf_op jit(solution)/shard_map/reduce_scatter | solution.py:236
  219.2 75.1 %copy-start.2 = (bf16[1,256,1024]{2,1,0:T(8,128)(2,1)S(1)}, bf16[1,256,1024]{2,1,0:T(8,128)(2,1)}, u32[]{:S(2)}) copy-start(bf16[1,256,1024]{2,1,0:T(8,128)(2,1)} %param.22) | copy-start | bytes 1572868
  224.1 3.5 copy-start
  233.2 3.5 copy-start
  242.3 4.7 copy-start
  252.7 3.5 copy-start
  270.9 3.5 copy-start
  280.1 3.5 copy-start
  293.6 11.5 copy-start.6
  297.1 57.5 %copy-start.17 = (bf16[1,256,1024]{2,1,0:T(8,128)(2,1)S(1)}, bf16[1,256,1024]{2,1,0:T(8,128)(2,1)}, u32[]{:S(2)}) copy-start(bf16[1,256,1024]{2,1,0:T(8,128)(2,1)} %param.23) | copy-start | bytes 1572868
  354.6 8.7 copy-start.25
  367.6 7.4 copy-start.19
  382.1 4.0 copy-start.1
  397.1 4.0 copy-start.1
  412.2 4.0 copy-start.1
  427.2 4.0 copy-start.1
  442.2 4.0 copy-start.1
  457.2 4.0 copy-start.1
  472.2 4.0 copy-start.1
  487.2 4.0 copy-start.1
  495.2 181.4 %reduce-scatter.10.cloned.1.call-start = ((), (), s32[]{:S(2)}) async-start(), calls=%async_computation.11 | async-start | bytes 4718592 | tf_op jit(solution)/shard_map/reduce_scatter | solution.py:233
  495.9 214.9 %reduce-scatter.16.cloned.1.call-start = ((), (), s32[]{:S(2)}) async-start(), calls=%async_computation.14 | async-start | bytes 2621440 | tf_op jit(solution)/shard_map/reduce_scatter | solution.py:257
  499.3 285.9 %reduce-scatter.18.cloned.1.call-start = ((), (), s32[]{:S(2)}) async-start(), calls=%async_computation.15 | async-start | bytes 10485760 | tf_op jit(solution)/shard_map/reduce_scatter | solution.py:260
  506.9 352.7 %reduce-scatter.20.cloned.1.call-start = ((), (), s32[]{:S(2)}) async-start(), calls=%async_computation.16 | async-start | bytes 10485760 | tf_op jit(solution)/shard_map/reduce_scatter | solution.py:263
  516.4 404.1 %reduce-scatter.14.cloned.1.call-start = ((), (), s32[]{:S(2)}) async-start(), calls=%async_computation.13 | async-start | bytes 7864320 | tf_op jit(solution)/shard_map/reduce_scatter | solution.py:254
  682.7 261.0 %reduce-scatter.22.cloned.1.call-start = ((), (), s32[]{:S(2)}) async-start(), calls=%async_computation.20 | async-start | bytes 327680
  682.8 5.6 copy-start.21
  690.9 427.6 %all-reduce.3.cloned.1.call-start = ((), (), s32[]{:S(2)}) async-start(), calls=%async_computation.21 | async-start | bytes 9437184 | tf_op jit(solution)/shard_map/psum | solution.py:272
  859.6 436.6 %all-gather.23.cloned.1.call-start = ((), (), s32[]{:S(2)}) async-start(), calls=%async_computation.19 | async-start | bytes 14155776 | tf_op jit(solution)/shard_map/all_gather | solution.py:23
  920.5 8.3 copy-start.12
  928.8 37.6 %copy-start.22 = (bf16[4,256]{1,0:T(4,128)(2,1)S(1)}, bf16[4,256]{1,0:T(4,128)(2,1)}, u32[]{:S(2)}) copy-start(bf16[4,256]{1,0:T(4,128)(2,1)} %param.29) | copy-start | bytes 6148
  928.8 37.6 %copy-start.23 = (f32[4,256]{1,0:T(4,128)S(1)}, f32[4,256]{1,0:T(4,128)}, u32[]{:S(2)}) copy-start(f32[4,256]{1,0:T(4,128)} %param.34) | copy-start | bytes 12292
  928.8 37.6 %copy-start.24 = (f32[4,256]{1,0:T(4,128)S(1)}, f32[4,256]{1,0:T(4,128)}, u32[]{:S(2)}) copy-start(f32[4,256]{1,0:T(4,128)} %param.39) | copy-start | bytes 12292
  930.3 192.6 %copy-start.3 = (bf16[1024,1024]{1,0:T(8,128)(2,1)S(1)}, bf16[1024,1024]{1,0:T(8,128)(2,1)}, u32[]{:S(2)}) copy-start(bf16[1024,1024]{1,0:T(8,128)(2,1)} %param.28) | copy-start | bytes 6291460
  1118.5 4.3 copy-start.8
  1122.9 11.3 copy-start.4
  1122.9 11.3 copy-start.9
  1122.9 11.3 copy-start.10
  1122.9 12.5 copy-start.14
  1296.2 7.4 copy-start.5
  (8 other events, 15.0 us)
Sparse Core Ops, SparseCore 0:
  9.6 49.0 all-gather.10
  64.9 73.4 all-gather.18
  141.1 71.6 all-gather.20
  214.2 20.8 all-gather.12
  236.5 58.2 all-gather.14
  296.2 58.3 all-gather.16
  495.3 88.3 reduce-scatter.11
  588.3 88.2 reduce-scatter.9
  679.7 31.1 reduce-scatter.15
  713.5 71.7 reduce-scatter.17
  787.8 71.7 reduce-scatter.19
  862.1 58.3 reduce-scatter.13
  923.5 20.0 reduce-scatter.21
  948.0 170.4 all-reduce.2
  1120.8 175.3 all-gather.22
